TPU v7x, 32 devices: a whole 2x2x4 slice. The times are simulated.
32 devices in a mesh: band: 4 (over x, core), row: 8 (over z, y).
Axes of the slice: x: 2, y: 2, z: 4, core: 2. Of those that a mesh axis runs over, the one named last changes fastest.
Arguments:
- shape_coupling_matrices: bfloat16 [512, 4, 128, 128], P('row'), may hold values from 0 to 0.00390625
- target_strip_index: int32 [512, 4], P('row'), may hold values from 0 to 511, as said below
- occupied_entries_per_strip: int32 [512], P('row'), may hold values from 1 to 4
- prior_leaving_energy: bfloat16 [4, 65536], P('band', 'row'), may hold values from 0.19921875 to 3
- facet_kelvins: float32 [65536], P('row'), may hold values from 0.6 to 1.6
- emitting_ability: float32 [4, 65536], P('band', 'row'), may hold values from 0.2 to 0.9
- centre_frequency: float32 [4], P('band'), may hold values from 0.28 to 6.3
- frequency_span: float32 [4], P('band'), may hold values from 0.5 to 1.5
- prescribed_power_density: float32 [65536], P('row'), may hold values from -6 to 6
Outputs:
- corrected_kelvins: float32 [65536], P('row')
- refreshed_leaving_energy: float32 [4, 65536], P('band', 'row')
Inputs may be any that keep to these rules, and one draw needn't show every extreme that they name: `target_strip_index`: of the 256 entries of one device's rows, exactly 32 name a column tile held by each index of row.
All inputs are finite; a program needn't handle non-finite values.
Results may differ from a plain program's by a relative error of at most 0.0003.
Values may be sent and summed in bfloat16 or wider, within the bound.
No kernel may reach another device: no remote copies, remote signals or barrier semaphores. Data moves between devices by JAX's collectives and lax.ppermute only.
A program may use at most 64 MiB of HBM per device.

v0:
```python
import jax
import jax.numpy as jnp
from jax import lax
from jax.sharding import PartitionSpec as P


def emitter_terms(centre_sample, frequency_spacing, facet_kelvins):
    return (
        frequency_spacing[:, None]
        * centre_sample[:, None] ** 3
        / jnp.expm1(centre_sample[:, None] / facet_kelvins[None, :])
    )


def on_device(
    shape_coupling_matrices,
    target_strip_index,
    occupied_entries_per_strip,
    prior_leaving_energy,
    facet_kelvins,
    emitting_ability,
    centre_frequency,
    frequency_span,
    prescribed_power_density,
):
    bands_here, facets_here = prior_leaving_energy.shape
    tile_rows, slot_count = target_strip_index.shape
    tile_size = shape_coupling_matrices.shape[2]
    entries = tile_rows * slot_count
    flat_cols = target_strip_index.reshape(entries)
    gathered = lax.all_gather(prior_leaving_energy, "row", axis=1, tiled=True)
    picked = gathered.reshape(bands_here, -1, tile_size)[:, flat_cols]
    picked = picked.reshape(bands_here, tile_rows, slot_count, tile_size)
    slot_used = (
        lax.broadcasted_iota(jnp.int32, (tile_rows, slot_count), 1)
        < occupied_entries_per_strip[:, None]
    )
    masked = jnp.where(slot_used[None, :, :, None], picked, jnp.zeros_like(picked))
    incoming = jnp.einsum(
        "rkij,brkj->bri", shape_coupling_matrices, masked, preferred_element_type=jnp.float32
    ).reshape(bands_here, facets_here)
    partial_terms = emitter_terms(centre_frequency, frequency_span, facet_kelvins)
    planck_sum = lax.psum(jnp.sum(partial_terms, 0), "band")
    energy_portion = partial_terms / planck_sum
    kelvins_third_power = facet_kelvins**3
    ideal_emitter_power = energy_portion * kelvins_third_power * facet_kelvins
    refreshed_leaving_energy = (
        emitting_ability * ideal_emitter_power + (1.0 - emitting_ability) * incoming
    )
    quotient = emitting_ability / (1.0 - emitting_ability)
    flux_part = jnp.sum(quotient * (ideal_emitter_power - refreshed_leaving_energy), 0)
    gradient_piece = jnp.sum(quotient * 4.0 * energy_portion * kelvins_third_power, 0)
    balance_power_density, power_gradient = lax.psum((flux_part, gradient_piece), "band")
    corrected_kelvins = (
        facet_kelvins - (balance_power_density - prescribed_power_density) / power_gradient
    )
    return (corrected_kelvins, refreshed_leaving_energy)


def solution(mesh):
    in_specs = (
        P("row", None, None, None),
        P("row", None),
        P("row"),
        P("band", "row"),
        P("row"),
        P("band", "row"),
        P("band"),
        P("band"),
        P("row"),
    )
    out_specs = (P("row"), P("band", "row"))
    return jax.shard_map(
        on_device, mesh=mesh, in_specs=in_specs, out_specs=out_specs, check_vma=False
    )
```

profile of v0, /device:TPU:0, one launch (start us, length us, event | category | flops | bytes accessed | tf_op | source)
XLA Modules:
  0.0 104.3 jit_solution(12224050853336227778)
XLA Ops:
  7.2 0.0 copy-start
  7.2 0.0 copy-start.1
  7.2 0.0 all-reduce.3.cloned.1.call-start
  8.5 0.8 broadcast_divide_fusion
  9.3 12.9 %psum.21 = f32[8192]{0:T(1024)S(1)} all-reduce(f32[8192]{0:T(1024)S(1)} %broadcast_divide_fusion), channel_id=1, replica_groups=mesh['band'=4,'row'=8] {'band'}, use_global_device_ids=true, to_apply=%region_0.1 | all-reduce | flops 8192 | bytes 65536 | tf_op jit(solution)/shard_map/psum | solution.py:43
  22.2 31.3 %all_gather.3 = bf16[1,65536]{1,0:T(2,128)(2,1)S(1)} all-gather(bf16[1,8192]{1,0:T(2,128)(2,1)} %param.12), channel_id=1, replica_groups=mesh['band'=4,'row'=8] {'row'}, dimensions={1}, use_global_device_ids=true | all-gather | bytes 147456 | tf_op jit(solution)/shard_map/all_gather | solution.py:31
  53.5 0.8 copy.11
  54.3 0.1 reshape.85
  54.4 0.7 iota_compare_fusion
  55.1 0.8 multiply_multiply_fusion.2
  55.9 0.8 reduce
  56.7 0.9 gather_fusion
  57.6 0.1 select_bitcast_fusion
  57.7 6.3 %subtract_multiply_fusion = (f32[1,8192]{1,0:T(1,128)}, f32[1,8192]{1,0:T(1,128)S(1)}, f32[1,8192]{1,0:T(1,128)}) fusion(f32[1,8192]{1,0:T(1,128)S(1)} %bitcast.36, f32[1,8192]{1,0:T(1,128)} %param.14, bf16[64,4,128,128]{3,2,1,0:T(8,128)(2,1)} %param.9, bf16[64,4,128,1]{2,1,0,3:T(4,128)(2,1)S(1)} %select_bitcast_fusion), kind=kOutput, calls=%fused_computation.10 | convolution fusion | flops 8445952 | bytes 8617984 | tf_op jit(solution)/shard_map/rkij,brkj->bri/dot_general | solution.py:39
  64.0 0.7 multiply_multiply_fusion.1
  64.7 0.0 all-reduce.3.cloned.1.call-update
  64.7 31.3 %all-reduce.3.cloned.1.call-done = (f32[8192]{0:T(1024)}, f32[8192]{0:T(1024)}) async-done(((f32[8192]{0:T(1024)}, f32[8192]{0:T(1024)}), (f32[8192]{0:T(1024)}, f32[8192]{0:T(1024)})) %all-reduce.3.cloned.1.call-update) | async-done | bytes 65552 | tf_op jit(solution)/shard_map/psum | solution.py:53
  96.0 0.0 copy-done
  96.0 0.0 copy-done.1
  96.0 1.4 %divide_subtract_fusion = f32[8192]{0:T(1024)} fusion(f32[8192]{0:T(1024)S(1)} %copy-done, f32[8192]{0:T(1024)} %get-tuple-element.2, f32[8192]{0:T(1024)} %get-tuple-element.3, f32[8192]{0:T(1024)S(1)} %copy-done.1), kind=kLoop, calls=%fused_computation.8 | loop fusion | flops 24576 | bytes 163840 | tf_op jit(solution)/shard_map/sub | solution.py:55
  (2 shorter events, 0.0 us)
Async XLA Ops:
  7.2 88.8 %copy-start = (f32[8192]{0:T(1024)S(1)}, f32[8192]{0:T(1024)}, u32[]{:S(2)}) copy-start(f32[8192]{0:T(1024)} %param.13) | copy-start | bytes 98308
  7.2 88.8 %copy-start.1 = (f32[8192]{0:T(1024)S(1)}, f32[8192]{0:T(1024)}, u32[]{:S(2)}) copy-start(f32[8192]{0:T(1024)} %param.17) | copy-start | bytes 98308
  7.2 88.8 %all-reduce.3.cloned.1.call-start = ((), (), s32[]{:S(2)}) async-start(), calls=%async_computation | async-start | bytes 131072 | tf_op jit(solution)/shard_map/psum | solution.py:53
Sparse Core Ops, SparseCore 0:
  64.8 31.1 all-reduce.2
where the time goes:
time: 105 us; the launch traced here: 104 us
  blocking collectives  44.2 us (42%)
  waiting for transfers between devices  31.3 us (30%)
  between operations  15.4 us (15%)
  matrix products  6.3 us (6%)
  other arithmetic  5.3 us (5%)
  local copies, waits for them, and re-layouts  1.74 us (2%)
    psum x1, waiting for transfers between devices, on_device(): lax.psum((flux_part, gradient_piece), 'band')  31.3 us
    all_gather x1, blocking collectives, on_device(): gathered = lax.all_gather(prior_leaving_energy, 'row', axis=1, tiled=True)  31.3 us
    psum x1, blocking collectives, on_device(): planck_sum = lax.psum(jnp.sum(partial_terms, 0), 'band')  12.9 us
    dot_general x1, matrix products, on_device(): jnp.einsum('rkij,brkj->bri', shape_coupling_matrices, masked, preferred_e...  6.3 us
  transfers between devices with their start and end apart: 1, of which 1 were waited for; matrix products, arithmetic and copies ran while one was open for 0% of the time, Pallas kernels for 0%

commit v1 on v0

--- a/solution.py
+++ b/solution.py
@@ -28,7 +28,14 @@
     tile_size = shape_coupling_matrices.shape[2]
     entries = tile_rows * slot_count
     flat_cols = target_strip_index.reshape(entries)
-    gathered = lax.all_gather(prior_leaving_energy, "row", axis=1, tiled=True)
+    size = lax.axis_size("row")
+    hops = [(i, (i + 1) % size) for i in range(size)]
+    parts = [prior_leaving_energy]
+    for stride in range(1, size):
+        parts = [lax.ppermute(parts[0], "row", hops), *parts]
+    whole = jnp.concatenate(parts, axis=1)
+    shift = (lax.axis_index("row") + 1) * parts[-1].shape[1]
+    gathered = jnp.roll(whole, shift, axis=1)
     picked = gathered.reshape(bands_here, -1, tile_size)[:, flat_cols]
     picked = picked.reshape(bands_here, tile_rows, slot_count, tile_size)
     slot_used = (

time: 105 us -> 107 us (1.019)
  blocking collectives: 44.2 us -> 10.3 us
  waiting for transfers between devices: 31.3 us -> 62.4 us
  starting transfers between devices: 0.04 us -> 3.13 us
  local copies, waits for them, and re-layouts: 1.74 us -> 4.73 us
    ppermute x0 -> x7, waiting for transfers between devices: none -> 33.6 us  [on_device(): parts = [lax.ppermute(parts[0], 'row', hops), *parts]]
    all_gather x1 -> x0, blocking collectives: 31.3 us -> none  [on_device(): gathered = lax.all_gather(prior_leaving_energy, 'row', axis=1, tiled=True)]
    ppermute x0 -> x7, starting transfers between devices: none -> 3.09 us  [on_device(): parts = [lax.ppermute(parts[0], 'row', hops), *parts]]
    psum x1, blocking collectives: 12.9 us -> 10.3 us  [on_device(): planck_sum = lax.psum(jnp.sum(partial_terms, 0), 'band')]
    psum x1, waiting for transfers between devices: 31.3 us -> 28.7 us  [on_device(): lax.psum((flux_part, gradient_piece), 'band')]
    unnamed x5 -> x20, local copies, waits for them, and re-layouts: 0.78 us -> 2.22 us
  transfers between devices with their start and end apart: 1 -> 8, of which waited for: 1 -> 7; matrix products, arithmetic and copies ran while one was open for 0% -> 3% of each run, Pallas kernels for 0% -> 0%
where the time goes in v1:
time: 107 us
  waiting for transfers between devices  62.4 us (58%)
  between operations  15.4 us (14%)
  blocking collectives  10.3 us (10%)
  matrix products  6.3 us (6%)
  local copies, waits for them, and re-layouts  4.73 us (4%)
  other arithmetic  4.52 us (4%)
  starting transfers between devices  3.13 us (3%)
    ppermute x7, waiting for transfers between devices, on_device(): parts = [lax.ppermute(parts[0], 'row', hops), *parts]  33.6 us
    psum x1, waiting for transfers between devices, on_device(): lax.psum((flux_part, gradient_piece), 'band')  28.7 us
    psum x1, blocking collectives, on_device(): planck_sum = lax.psum(jnp.sum(partial_terms, 0), 'band')  10.3 us
    dot_general x1, matrix products, on_device(): jnp.einsum('rkij,brkj->bri', shape_coupling_matrices, masked, preferred_e...  6.3 us
    ppermute x7, starting transfers between devices, on_device(): parts = [lax.ppermute(parts[0], 'row', hops), *parts]  3.09 us
    unnamed x20, local copies, waits for them, and re-layouts  2.22 us
  transfers between devices with their start and end apart: 8, of which 7 were waited for; matrix products, arithmetic and copies ran while one was open for 3% of the time, Pallas kernels for 0%

profile of v1, /device:TPU:0, one launch (start us, length us, event | category | flops | bytes accessed | tf_op | source)
XLA Modules:
  0.0 106.8 jit_solution(1032484052199541190)
XLA Ops:
  7.2 0.0 copy-start
  7.2 0.0 copy-start.1
  7.2 0.0 all-reduce.3.cloned.1.call-start
  7.2 3.0 %collective-permute-start = (bf16[1,8192]{1,0:T(2,128)(2,1)}, bf16[1,8192]{1,0:T(2,128)(2,1)S(1)}, u32[]{:S(2)}, u32[]{:S(2)}) collective-permute-start(bf16[1,8192]{1,0:T(2,128)(2,1)} %param.12), channel_id=1, source_target_pairs={{0,1},{1,2},{2,3},{3,4},{4,5},{5,6},{6,7},{7,0},{8,9},{9,10},{10,1... | collective-permute-start | bytes 49160 | tf_op jit(solution)/shard_map/ppermute | solution.py:35
  11.6 3.8 %collective-permute-done = bf16[1,8192]{1,0:T(2,128)(2,1)S(1)} collective-permute-done((bf16[1,8192]{1,0:T(2,128)(2,1)}, bf16[1,8192]{1,0:T(2,128)(2,1)S(1)}, u32[]{:S(2)}, u32[]{:S(2)}) %collective-permute-start) | collective-permute-done | bytes 16416 | tf_op jit(solution)/shard_map/ppermute | solution.py:35
  15.4 0.0 collective-permute-start.1
  15.4 0.8 broadcast_divide_fusion
  16.2 5.8 %collective-permute-done.1 = bf16[1,8192]{1,0:T(2,128)(2,1)S(1)} collective-permute-done((bf16[1,8192]{1,0:T(2,128)(2,1)S(1)}, bf16[1,8192]{1,0:T(2,128)(2,1)S(1)}, u32[]{:S(2)}, u32[]{:S(2)}) %collective-permute-start.1) | collective-permute-done | bytes 16416 | tf_op jit(solution)/shard_map/ppermute | solution.py:35
  22.0 0.0 collective-permute-start.2
  22.0 10.3 %psum.21 = f32[8192]{0:T(1024)S(1)} all-reduce(f32[8192]{0:T(1024)S(1)} %broadcast_divide_fusion), channel_id=1, replica_groups=mesh['band'=4,'row'=8] {'band'}, use_global_device_ids=true, to_apply=%region_0.1 | all-reduce | flops 8192 | bytes 65536 | tf_op jit(solution)/shard_map/psum | solution.py:50
  32.3 0.0 collective-permute-done.2
  32.3 0.1 collective-permute-start.3
  32.3 0.8 multiply_multiply_fusion.2
  33.1 5.8 %collective-permute-done.3 = bf16[1,8192]{1,0:T(2,128)(2,1)S(1)} collective-permute-done((bf16[1,8192]{1,0:T(2,128)(2,1)S(1)}, bf16[1,8192]{1,0:T(2,128)(2,1)S(1)}, u32[]{:S(2)}, u32[]{:S(2)}) %collective-permute-start.3) | collective-permute-done | bytes 16416 | tf_op jit(solution)/shard_map/ppermute | solution.py:35
  39.0 0.0 collective-permute-start.4
  39.0 0.7 iota_compare_fusion
  39.7 0.8 copy.11
  40.5 0.1 reshape.85
  40.6 5.0 %collective-permute-done.4 = bf16[1,8192]{1,0:T(2,128)(2,1)S(1)} collective-permute-done((bf16[1,8192]{1,0:T(2,128)(2,1)S(1)}, bf16[1,8192]{1,0:T(2,128)(2,1)S(1)}, u32[]{:S(2)}, u32[]{:S(2)}) %collective-permute-start.4) | collective-permute-done | bytes 16416 | tf_op jit(solution)/shard_map/ppermute | solution.py:35
  45.6 0.0 collective-permute-start.5
  45.6 6.6 %collective-permute-done.5 = bf16[1,8192]{1,0:T(2,128)(2,1)S(1)} collective-permute-done((bf16[1,8192]{1,0:T(2,128)(2,1)S(1)}, bf16[1,8192]{1,0:T(2,128)(2,1)S(1)}, u32[]{:S(2)}, u32[]{:S(2)}) %collective-permute-start.5) | collective-permute-done | bytes 16416 | tf_op jit(solution)/shard_map/ppermute | solution.py:35
  52.2 0.0 collective-permute-start.6
  52.2 6.6 %collective-permute-done.6 = bf16[1,8192]{1,0:T(2,128)(2,1)S(1)} collective-permute-done((bf16[1,8192]{1,0:T(2,128)(2,1)S(1)}, bf16[1,8192]{1,0:T(2,128)(2,1)S(1)}, u32[]{:S(2)}, u32[]{:S(2)}) %collective-permute-start.6) | collective-permute-done | bytes 16416 | tf_op jit(solution)/shard_map/ppermute | solution.py:35
  59.1 0.8 constant_dynamic-update-slice_fusion.8
  60.2 0.8 constant_dynamic-update-slice_fusion
  61.0 0.7 dynamic-slice_reduce_fusion
  61.8 0.9 gather_fusion
  62.6 0.1 select_bitcast_fusion
  62.8 6.3 %subtract_multiply_fusion = (f32[1,8192]{1,0:T(1,128)}, f32[1,8192]{1,0:T(1,128)S(1)}, f32[1,8192]{1,0:T(1,128)}) fusion(f32[1,8192]{1,0:T(1,128)S(1)} %bitcast.36, f32[1,8192]{1,0:T(1,128)} %param.14, bf16[64,4,128,128]{3,2,1,0:T(8,128)(2,1)} %param.9, bf16[64,4,128,1]{2,1,0,3:T(4,128)(2,1)S(1)} %select_bitcast_fusion), kind=kOutput, calls=%fused_computation.27 | convolution fusion | flops 8445952 | bytes 8617984 | tf_op jit(solution)/shard_map/rkij,brkj->bri/dot_general | solution.py:46
  69.1 0.7 multiply_multiply_fusion.1
  69.7 0.0 all-reduce.3.cloned.1.call-update
  69.8 28.7 %all-reduce.3.cloned.1.call-done = (f32[8192]{0:T(1024)}, f32[8192]{0:T(1024)}) async-done(((f32[8192]{0:T(1024)}, f32[8192]{0:T(1024)}), (f32[8192]{0:T(1024)}, f32[8192]{0:T(1024)})) %all-reduce.3.cloned.1.call-update) | async-done | bytes 65552 | tf_op jit(solution)/shard_map/psum | solution.py:60
  98.5 0.0 copy-done
  98.5 0.0 copy-done.1
  98.5 1.4 %divide_subtract_fusion = f32[8192]{0:T(1024)} fusion(f32[8192]{0:T(1024)S(1)} %copy-done, f32[8192]{0:T(1024)} %get-tuple-element.2, f32[8192]{0:T(1024)} %get-tuple-element.3, f32[8192]{0:T(1024)S(1)} %copy-done.1), kind=kLoop, calls=%fused_computation.25 | loop fusion | flops 24576 | bytes 163840 | tf_op jit(solution)/shard_map/sub | solution.py:62
  (16 shorter events, 0.6 us)
Async XLA Ops:
  7.2 91.3 %copy-start = (f32[8192]{0:T(1024)S(1)}, f32[8192]{0:T(1024)}, u32[]{:S(2)}) copy-start(f32[8192]{0:T(1024)} %param.13) | copy-start | bytes 98308
  7.2 91.3 %copy-start.1 = (f32[8192]{0:T(1024)S(1)}, f32[8192]{0:T(1024)}, u32[]{:S(2)}) copy-start(f32[8192]{0:T(1024)} %param.17) | copy-start | bytes 98308
  7.2 91.3 %all-reduce.3.cloned.1.call-start = ((), (), s32[]{:S(2)}) async-start(), calls=%async_computation | async-start | bytes 131072 | tf_op jit(solution)/shard_map/psum | solution.py:60
  7.2 8.2 %collective-permute-start = (bf16[1,8192]{1,0:T(2,128)(2,1)}, bf16[1,8192]{1,0:T(2,128)(2,1)S(1)}, u32[]{:S(2)}, u32[]{:S(2)}) collective-permute-start(bf16[1,8192]{1,0:T(2,128)(2,1)} %param.12), channel_id=1, source_target_pairs={{0,1},{1,2},{2,3},{3,4},{4,5},{5,6},{6,7},{7,0},{8,9},{9,10},{10,1... | collective-permute-start | bytes 49160 | tf_op jit(solution)/shard_map/ppermute | solution.py:35
  15.4 6.6 %collective-permute-start.1 = (bf16[1,8192]{1,0:T(2,128)(2,1)S(1)}, bf16[1,8192]{1,0:T(2,128)(2,1)S(1)}, u32[]{:S(2)}, u32[]{:S(2)}) collective-permute-start(bf16[1,8192]{1,0:T(2,128)(2,1)S(1)} %collective-permute-done), channel_id=1, source_target_pairs={{0,1},{1,2},{2,3},{3,4},{4,5},{5,6},{6,7},{7,0},{8,9},{9,10},{10,1... | collective-permute-start | bytes 49160 | tf_op jit(solution)/shard_map/ppermute | solution.py:35
  22.0 10.3 %collective-permute-start.2 = (bf16[1,8192]{1,0:T(2,128)(2,1)S(1)}, bf16[1,8192]{1,0:T(2,128)(2,1)S(1)}, u32[]{:S(2)}, u32[]{:S(2)}) collective-permute-start(bf16[1,8192]{1,0:T(2,128)(2,1)S(1)} %collective-permute-done.1), channel_id=1, source_target_pairs={{0,1},{1,2},{2,3},{3,4},{4,5},{5,6},{6,7},{7,0},{8,9},{9,10},{10,1... | collective-permute-start | bytes 49160 | tf_op jit(solution)/shard_map/ppermute | solution.py:35
  32.3 6.7 %collective-permute-start.3 = (bf16[1,8192]{1,0:T(2,128)(2,1)S(1)}, bf16[1,8192]{1,0:T(2,128)(2,1)S(1)}, u32[]{:S(2)}, u32[]{:S(2)}) collective-permute-start(bf16[1,8192]{1,0:T(2,128)(2,1)S(1)} %collective-permute-done.2), channel_id=1, source_target_pairs={{0,1},{1,2},{2,3},{3,4},{4,5},{5,6},{6,7},{7,0},{8,9},{9,10},{10,1... | collective-permute-start | bytes 49160 | tf_op jit(solution)/shard_map/ppermute | solution.py:35
  39.0 6.6 %collective-permute-start.4 = (bf16[1,8192]{1,0:T(2,128)(2,1)S(1)}, bf16[1,8192]{1,0:T(2,128)(2,1)S(1)}, u32[]{:S(2)}, u32[]{:S(2)}) collective-permute-start(bf16[1,8192]{1,0:T(2,128)(2,1)S(1)} %collective-permute-done.3), channel_id=1, source_target_pairs={{0,1},{1,2},{2,3},{3,4},{4,5},{5,6},{6,7},{7,0},{8,9},{9,10},{10,1... | collective-permute-start | bytes 49160 | tf_op jit(solution)/shard_map/ppermute | solution.py:35
  45.6 6.6 %collective-permute-start.5 = (bf16[1,8192]{1,0:T(2,128)(2,1)S(1)}, bf16[1,8192]{1,0:T(2,128)(2,1)S(1)}, u32[]{:S(2)}, u32[]{:S(2)}) collective-permute-start(bf16[1,8192]{1,0:T(2,128)(2,1)S(1)} %collective-permute-done.4), channel_id=1, source_target_pairs={{0,1},{1,2},{2,3},{3,4},{4,5},{5,6},{6,7},{7,0},{8,9},{9,10},{10,1... | collective-permute-start | bytes 49160 | tf_op jit(solution)/shard_map/ppermute | solution.py:35
  52.2 6.6 %collective-permute-start.6 = (bf16[1,8192]{1,0:T(2,128)(2,1)S(1)}, bf16[1,8192]{1,0:T(2,128)(2,1)S(1)}, u32[]{:S(2)}, u32[]{:S(2)}) collective-permute-start(bf16[1,8192]{1,0:T(2,128)(2,1)S(1)} %collective-permute-done.5), channel_id=1, source_target_pairs={{0,1},{1,2},{2,3},{3,4},{4,5},{5,6},{6,7},{7,0},{8,9},{9,10},{10,1... | collective-permute-start | bytes 49160 | tf_op jit(solution)/shard_map/ppermute | solution.py:35
Sparse Core Ops, SparseCore 0:
  69.9 28.5 all-reduce.2

commit v2 on v0

--- a/solution.py
+++ b/solution.py
@@ -1,7 +1,16 @@
+import functools
 import jax
 import jax.numpy as jnp
 from jax import lax
 from jax.sharding import PartitionSpec as P
+
+
+def carry_the_stops_all(obj, chip_axis):
+    a_next = lax.all_gather(obj, axis_name=chip_axis).sum(axis=0)
+    return a_next
+
+
+orders_report = functools.partial(carry_the_stops_all, chip_axis="band")
 
 
 def emitter_terms(centre_sample, frequency_spacing, facet_kelvins):
@@ -40,7 +49,7 @@
         "rkij,brkj->bri", shape_coupling_matrices, masked, preferred_element_type=jnp.float32
     ).reshape(bands_here, facets_here)
     partial_terms = emitter_terms(centre_frequency, frequency_span, facet_kelvins)
-    planck_sum = lax.psum(jnp.sum(partial_terms, 0), "band")
+    planck_sum = orders_report(jnp.sum(partial_terms, 0))
     energy_portion = partial_terms / planck_sum
     kelvins_third_power = facet_kelvins**3
     ideal_emitter_power = energy_portion * kelvins_third_power * facet_kelvins

time: 105 us -> 99.8 us (0.950)
  blocking collectives: 44.2 us -> 38.3 us
    psum x1 -> x0, blocking collectives: 12.9 us -> none  [on_device(): planck_sum = lax.psum(jnp.sum(partial_terms, 0), 'band')]
    all_gather x0 -> x1, blocking collectives: none -> 6.48 us  [carry_the_stops_all(): a_next = lax.all_gather(obj, axis_name=chip_axis).sum(axis=0)]
where the time goes in v2:
time: 99.8 us; the launch traced here: 99.3 us
  blocking collectives  38.3 us (38%)
  waiting for transfers between devices  32.1 us (32%)
  between operations  15.4 us (15%)
  matrix products  6.3 us (6%)
  other arithmetic  5.37 us (5%)
  local copies, waits for them, and re-layouts  1.79 us (2%)
    psum x1, waiting for transfers between devices, on_device(): lax.psum((flux_part, gradient_piece), 'band')  32.1 us
    all_gather x1, blocking collectives, on_device(): gathered = lax.all_gather(prior_leaving_energy, 'row', axis=1, tiled=True)  31.8 us
    all_gather x1, blocking collectives, carry_the_stops_all(): a_next = lax.all_gather(obj, axis_name=chip_axis).sum(axis=0)  6.48 us
    dot_general x1, matrix products, on_device(): jnp.einsum('rkij,brkj->bri', shape_coupling_matrices, masked, preferred_e...  6.3 us
  transfers between devices with their start and end apart: 1, of which 1 were waited for; matrix products, arithmetic and copies ran while one was open for 0% of the time, Pallas kernels for 0%

profile of v2, /device:TPU:0, one launch (start us, length us, event | category | flops | bytes accessed | tf_op | source)
XLA Modules:
  0.0 99.3 jit_solution(7757648280148859822)
XLA Ops:
  7.2 0.0 copy-start
  7.2 0.0 copy-start.1
  7.2 0.0 all-reduce.3.cloned.1.call-start
  8.5 0.8 broadcast_divide_fusion
  9.3 6.5 %all-gather = f32[32768]{0:T(1024)S(1)} all-gather(f32[8192]{0:T(1024)S(1)} %broadcast_divide_fusion), channel_id=2, replica_groups=mesh['band'=4,'row'=8] {'band'}, dimensions={0}, use_global_device_ids=true | all-gather | bytes 163840 | tf_op jit(solution)/shard_map/all_gather | solution.py:9
  15.9 31.8 %all_gather.8 = bf16[1,65536]{1,0:T(2,128)(2,1)S(1)} all-gather(bf16[1,8192]{1,0:T(2,128)(2,1)} %param.12), channel_id=1, replica_groups=mesh['band'=4,'row'=8] {'row'}, dimensions={1}, use_global_device_ids=true | all-gather | bytes 147456 | tf_op jit(solution)/shard_map/all_gather | solution.py:40
  47.7 0.8 copy.13
  48.4 0.1 reshape.85
  48.6 0.7 iota_compare_fusion
  49.3 0.1 reduce_sum.15
  49.4 0.8 multiply_multiply_fusion.2
  50.2 0.8 reduce
  51.0 0.9 gather_fusion
  51.8 0.1 select_bitcast_fusion
  52.0 6.3 %subtract_multiply_fusion = (f32[1,8192]{1,0:T(1,128)}, f32[1,8192]{1,0:T(1,128)S(1)}, f32[1,8192]{1,0:T(1,128)}) fusion(f32[1,8192]{1,0:T(1,128)S(1)} %bitcast.36, f32[1,8192]{1,0:T(1,128)} %param.14, bf16[64,4,128,128]{3,2,1,0:T(8,128)(2,1)} %param.9, bf16[64,4,128,1]{2,1,0,3:T(4,128)(2,1)S(1)} %select_bitcast_fusion), kind=kOutput, calls=%fused_computation.10 | convolution fusion | flops 8445952 | bytes 8617984 | tf_op jit(solution)/shard_map/rkij,brkj->bri/dot_general | solution.py:48
  58.3 0.7 multiply_multiply_fusion.1
  58.9 0.0 all-reduce.3.cloned.1.call-update
  59.0 32.1 %all-reduce.3.cloned.1.call-done = (f32[8192]{0:T(1024)}, f32[8192]{0:T(1024)}) async-done(((f32[8192]{0:T(1024)}, f32[8192]{0:T(1024)}), (f32[8192]{0:T(1024)}, f32[8192]{0:T(1024)})) %all-reduce.3.cloned.1.call-update) | async-done | bytes 65552 | tf_op jit(solution)/shard_map/psum | solution.py:62
  91.1 0.0 copy-done
  91.1 0.0 copy-done.1
  91.1 1.4 %divide_subtract_fusion = f32[8192]{0:T(1024)} fusion(f32[8192]{0:T(1024)S(1)} %copy-done, f32[8192]{0:T(1024)} %get-tuple-element.2, f32[8192]{0:T(1024)} %get-tuple-element.3, f32[8192]{0:T(1024)S(1)} %copy-done.1), kind=kLoop, calls=%fused_computation.8 | loop fusion | flops 24576 | bytes 163840 | tf_op jit(solution)/shard_map/sub | solution.py:64
  (3 shorter events, 0.1 us)
Async XLA Ops:
  7.2 83.9 %copy-start = (f32[8192]{0:T(1024)S(1)}, f32[8192]{0:T(1024)}, u32[]{:S(2)}) copy-start(f32[8192]{0:T(1024)} %param.13) | copy-start | bytes 98308
  7.2 83.9 %copy-start.1 = (f32[8192]{0:T(1024)S(1)}, f32[8192]{0:T(1024)}, u32[]{:S(2)}) copy-start(f32[8192]{0:T(1024)} %param.17) | copy-start | bytes 98308
  7.2 83.9 %all-reduce.3.cloned.1.call-start = ((), (), s32[]{:S(2)}) async-start(), calls=%async_computation | async-start | bytes 131072 | tf_op jit(solution)/shard_map/psum | solution.py:62
Sparse Core Ops, SparseCore 0:
  59.1 31.9 all-reduce.2
